TPU v7x, 32 devices: a whole 2x2x4 slice. The times are simulated.
32 devices in a mesh: gx: 4 (over x, core), gy: 8 (over z, y).
Axes of the slice: x: 2, y: 2, z: 4, core: 2. Of those that a mesh axis runs over, the one named last changes fastest.
Arguments:
- adjoint: float32 [2, 256, 768, 128], P(None, 'gx', 'gy'), may hold values from -6 to 6
- medium: bfloat16 [5, 256, 768, 128], P(None, 'gx', 'gy'), may hold values from -4 to 4, as said below
- rotors: float32 [4, 2048], P(None, ('gx', 'gy')), may hold values from -0.5 to 2
- step_size: float32 [], replicated, may hold values from 0.02 to 0.1
- slot_turbine: int32 [6144], P(('gx', 'gy')), may hold values from -1 to 2047, as said below
- slot_corner: int32 [3, 6144], P(None, ('gx', 'gy')), may hold values from 0 to 112, as said below
- moved_rotors: int32 [128], P(('gx', 'gy')), may hold values from 0 to 63, as said below
- new_brick: int32 [128, 1], P(('gx', 'gy')), may hold values from 0 to 31; in each aligned block of 128 rows (0 to 127, 128 to 255, ...) at most 8 rows name the same one
Outputs:
- adjoint_out: float32 [2, 256, 768, 128], P(None, 'gx', 'gy')
- step_taken: float32 [2, 2048], P(None, ('gx', 'gy'))
- incoming: bfloat16 [256, 2048], P(('gx', 'gy'))
Inputs may be any that keep to these rules, and one draw needn't show every extreme that they name: `slot_turbine`: entries are global turbine numbers or -1 for an empty slot. Every turbine is listed exactly once over all bricks. A brick lists at most 192 turbines, and some brick lists exactly 192. `slot_corner`: every listed block of 8 x 16 x 16 cells lies inside its brick. `moved_rotors`: the 4 entries of one owner are distinct. `new_brick`: over all moved rotors, no brick is named more than 8 times, a bound that some block reaches. `medium`: viscosity in 0.1 to 1, velocity in 0.2 to 1, dissipation in 0.1 to 1, coupling in -0.3 to 0.3, source in -4 to 4.
All inputs are finite; a program needn't handle non-finite values.
Results may differ from a plain program's by a relative error of at most 0.001.
Values may be sent and summed in bfloat16 or wider, within the bound.
A program may use at most 256 MiB of HBM per device.

v0:
```python
import functools

import jax
import jax.numpy as jnp
import numpy as np
from jax import lax
from jax.experimental import pallas as pl
from jax.experimental.pallas import tpu as pltpu
from jax.sharding import PartitionSpec as P

KX = 8
KY = 16
KZ = 16
SWEEPS = 2
RECV = 8
EDGE = 16
CHUNK = 8
LANES = 128


TAU = 0.05
SIGMA_AXIAL = 1.5
SIGMA_RADIAL = 4.0
MESH = pl.DeviceIdType.MESH


def sweep_plane(med, src, dst, prev, x, count):
    ahead = jnp.minimum(x + 1, count - 1)
    inside = jnp.where(x + 1 < count, 1.0, 0.0)
    viscous = med[0, x].astype(jnp.float32)
    velocity = med[1, x].astype(jnp.float32)
    reaction = med[2, x].astype(jnp.float32)
    coupling = med[3, x].astype(jnp.float32)
    source = med[4, x].astype(jnp.float32)
    pull = (med[0, ahead].astype(jnp.float32) + med[1, ahead].astype(jnp.float32)) * inside
    diagonal = 6.0 * viscous + velocity + reaction
    rows, cols = viscous.shape
    row = lax.broadcasted_iota(jnp.int32, (rows, cols), 0)
    col = lax.broadcasted_iota(jnp.int32, (rows, cols), 1)
    sides = []
    for c in range(2):
        flux = viscous * src[c, x]
        total = prev[c] + pull * src[c, ahead]
        prev[c] = flux
        total = total + jnp.where(row == 0, 0.0, pltpu.roll(flux, 1, 0))
        total = total + jnp.where(row == rows - 1, 0.0, pltpu.roll(flux, rows - 1, 0))
        total = total + jnp.where(col == 0, 0.0, pltpu.roll(flux, 1, 1))
        total = total + jnp.where(col == cols - 1, 0.0, pltpu.roll(flux, cols - 1, 1))
        sides.append(total)
    k, e = src[0, x], src[1, x]
    dst[0, x] = k + TAU * (source + sides[0] - diagonal * k - coupling * e)
    dst[1, x] = e + TAU * (sides[1] - (diagonal + reaction) * e - coupling * k)


def relax_kernel(
    sizes, q_hbm, med_hbm, out_hbm, q, med, q1, prev, xs, xr, ys, yr, edge_sem, in_sem, out_sem, ssem, rsem
):
    n_gx, n_gy = sizes
    _, count, width, _ = q.shape
    chunks = count // CHUNK
    gx, gy = lax.axis_index("gx"), lax.axis_index("gy")
    x_lo, x_hi = lax.rem(gx + n_gx - 1, n_gx), lax.rem(gx + 1, n_gx)
    y_lo, y_hi = lax.rem(gy + n_gy - 1, n_gy), lax.rem(gy + 1, n_gy)
    peers = ((x_lo, gy), (x_hi, gy), (gx, y_lo), (gx, y_hi))
    mid = pl.ds(EDGE, width - 2 * EDGE)
    edges = (pl.ds(0, EDGE), pl.ds(width - EDGE, EDGE))

    edge_in = []
    for i, part in enumerate(edges):
        edge_in.append(pltpu.make_async_copy(q_hbm.at[:, :, part], q.at[:, :, part], edge_sem.at[i, 0]))
        edge_in.append(
            pltpu.make_async_copy(med_hbm.at[0, :, part], med.at[0, :, part], edge_sem.at[i, 1])
        )

    def chunk_in(i):
        part = pl.ds(i * CHUNK, CHUNK)
        return (
            pltpu.make_async_copy(q_hbm.at[:, part, mid], q.at[:, part, mid], in_sem.at[i, 0]),
            pltpu.make_async_copy(med_hbm.at[0, part, mid], med.at[0, part, mid], in_sem.at[i, 1]),
            pltpu.make_async_copy(
                med_hbm.at[pl.ds(1, 4), part], med.at[pl.ds(1, 4), part], in_sem.at[i, 2]
            ),
        )

    for copy in edge_in:
        copy.start()
    for i in [0, chunks - 1] + list(range(1, chunks - 1)):
        for copy in chunk_in(i):
            copy.start()

    barrier = pltpu.get_barrier_semaphore()
    for peer in peers:
        pl.semaphore_signal(barrier, inc=1, device_id=peer, device_id_type=MESH)
    pl.semaphore_wait(barrier, 4)

    def exchange(turn, src):
        for c in range(2):
            low, high = med[0, 0].astype(jnp.float32), med[0, count - 1].astype(jnp.float32)
            xs[turn, 0, c] = (low + med[1, 0].astype(jnp.float32)) * src[c, 0]
            xs[turn, 1, c] = high * src[c, count - 1]

        copies = []
        for side in range(2):
            copies.append(
                pltpu.make_async_remote_copy(
                    src_ref=xs.at[turn, side],
                    dst_ref=xr.at[turn, side],
                    send_sem=ssem.at[turn, side],
                    recv_sem=rsem.at[turn, side],
                    device_id=peers[side],
                    device_id_type=MESH,
                )
            )
            copies[-1].start()

        @pl.loop(0, count, unroll=4)
        def _(x):
            low = med[0, x, pl.ds(0, EDGE)].astype(jnp.float32)[:8]
            high = med[0, x, pl.ds(width - EDGE, EDGE)].astype(jnp.float32)[8:]
            for c in range(2):
                ys[turn, 0, c, pl.ds(x, 1)] = (low * src[c, x, pl.ds(0, 8)])[:1]
                ys[turn, 1, c, pl.ds(x, 1)] = (high * src[c, x, pl.ds(width - 8, 8)])[7:]

        for side in range(2):
            copies.append(
                pltpu.make_async_remote_copy(
                    src_ref=ys.at[turn, side],
                    dst_ref=yr.at[turn, side],
                    send_sem=ssem.at[turn, 2 + side],
                    recv_sem=rsem.at[turn, 2 + side],
                    device_id=peers[2 + side],
                    device_id_type=MESH,
                )
            )
            copies[-1].start()
        return copies

    def patch(turn, dst):
        has_hi_x = jnp.where(gx < n_gx - 1, TAU, 0.0)
        has_lo_x = jnp.where(gx > 0, TAU, 0.0)
        has_hi_y = jnp.where(gy < n_gy - 1, TAU, 0.0)
        has_lo_y = jnp.where(gy > 0, TAU, 0.0)
        for c in range(2):
            dst[c, count - 1] = dst[c, count - 1] + has_hi_x * xr[turn, 0, c]
            dst[c, 0] = dst[c, 0] + has_lo_x * xr[turn, 1, c]

        @pl.loop(0, count, unroll=4)
        def _(x):
            for c in range(2):
                last = pl.ds(width - 1, 1)
                first = pl.ds(0, 1)
                dst[c, x, last] = dst[c, x, last] + has_hi_y * yr[turn, 0, c, pl.ds(x, 1)]
                dst[c, x, first] = dst[c, x, first] + has_lo_y * yr[turn, 1, c, pl.ds(x, 1)]

    for copy in edge_in:
        copy.wait()
    for i in (0, chunks - 1):
        for copy in chunk_in(i):
            copy.wait()

    copies = exchange(0, q)
    prev[...] = jnp.zeros_like(prev)
    for i in range(chunks):
        if 0 < i + 1 < chunks - 1:
            for copy in chunk_in(i + 1):
                copy.wait()

        @pl.loop(0, CHUNK)
        def _(j):
            sweep_plane(med, q, q1, prev, i * CHUNK + j, count)

    for copy in copies:
        copy.wait()
    patch(0, q1)

    copies = exchange(1, q1)
    prev[...] = jnp.zeros_like(prev)

    def chunk_out(i):
        part = pl.ds(i * CHUNK, CHUNK)
        return pltpu.make_async_copy(q.at[:, part, mid], out_hbm.at[:, part, mid], out_sem.at[i])

    outs = []
    for i in range(chunks):

        @pl.loop(0, CHUNK)
        def _(j):
            sweep_plane(med, q1, q, prev, i * CHUNK + j, count)

        if 0 < i < chunks - 1:
            outs.append(chunk_out(i))
            outs[-1].start()

    for copy in copies:
        copy.wait()
    patch(1, q)
    tail = [chunk_out(0), chunk_out(chunks - 1)]
    for i, part in enumerate(edges):
        sem = out_sem.at[chunks + i]
        tail.append(pltpu.make_async_copy(q.at[:, :, part], out_hbm.at[:, :, part], sem))
    for copy in tail:
        copy.start()
    for copy in outs + tail:
        copy.wait()


def relax(adjoint, medium, sizes):
    channels, count, width, depth = adjoint.shape
    return pl.pallas_call(
        functools.partial(relax_kernel, sizes),
        out_shape=jax.ShapeDtypeStruct(adjoint.shape, jnp.float32),
        in_specs=[pl.BlockSpec(memory_space=pl.ANY)] * 2,
        out_specs=pl.BlockSpec(memory_space=pl.ANY),
        scratch_shapes=[
            pltpu.VMEM(adjoint.shape, jnp.float32),
            pltpu.VMEM(medium.shape, jnp.bfloat16),
            pltpu.VMEM(adjoint.shape, jnp.float32),
            pltpu.VMEM((channels, width, depth), jnp.float32),
            pltpu.VMEM((2, 2, channels, width, depth), jnp.float32),
            pltpu.VMEM((2, 2, channels, width, depth), jnp.float32),
            pltpu.VMEM((2, 2, channels, count, depth), jnp.float32),
            pltpu.VMEM((2, 2, channels, count, depth), jnp.float32),
            pltpu.SemaphoreType.DMA((2, 2)),
            pltpu.SemaphoreType.DMA((count // CHUNK, 3)),
            pltpu.SemaphoreType.DMA((2 + count // CHUNK,)),
            pltpu.SemaphoreType.DMA((2, 4)),
            pltpu.SemaphoreType.DMA((2, 4)),
        ],
        compiler_params=pltpu.CompilerParams(
            collective_id=0, has_side_effects=True, vmem_limit_bytes=48 * 1024 * 1024
        ),
        name="relax",
    )(adjoint, medium)


def z_weights(depth):
    z = np.arange(depth)[:, None] - np.arange(depth)[None, :]
    height = z + 0.5 - KZ / 2.0
    values = np.exp(-(height**2) / (2.0 * SIGMA_RADIAL**2)) * ((z >= 0) & (z < KZ))
    values = values.astype(np.float32)
    high = values.astype(jnp.bfloat16)
    low = (values - high.astype(np.float32)).astype(jnp.bfloat16)
    return np.block([[high, low], [high, np.zeros_like(low)]])


def slope_kernel(
    turb_dev, slot_turbine, corner, table, q_hbm, profile, out_hbm, slopes, q, conv, in_sem, out_sem
):
    _, count, width, depth = q.shape
    chunks = count // CHUNK
    slots = slot_turbine.shape[0]

    def chunk_in(i):
        part = pl.ds(i * CHUNK, CHUNK)
        return pltpu.make_async_copy(q_hbm.at[:, part], q.at[:, part], in_sem.at[i])

    def chunk_out(i):
        part = pl.ds(i * CHUNK, CHUNK)
        return pltpu.make_async_copy(q.at[:, part], out_hbm.at[:, part], out_sem.at[i])

    for i in range(chunks):
        chunk_in(i).start()
    for i in range(chunks):
        chunk_in(i).wait()
        chunk_out(i).start()
        rows = q[0, pl.ds(i * CHUNK, CHUNK)].reshape(CHUNK * width, depth)
        high = rows.astype(jnp.bfloat16)
        low = (rows - high.astype(jnp.float32)).astype(jnp.bfloat16)
        both = jnp.dot(
            jnp.concatenate([high, low], axis=1),
            profile[...],
            preferred_element_type=jnp.float32,
        )
        conv[pl.ds(i * CHUNK, CHUNK)] = (both[:, :depth] + both[:, depth:]).reshape(
            CHUNK, width, depth
        )

    lane = lax.broadcasted_iota(jnp.int32, (1, LANES), 1)
    wide = lax.broadcasted_iota(jnp.int32, (KX * KY, LANES), 1)
    cell = lax.broadcasted_iota(jnp.int32, (KX * KY, LANES), 0)
    cell_x = (cell // KY).astype(jnp.float32) + 0.5 - KX / 2.0
    cell_y = lax.rem(cell, KY).astype(jnp.float32) + 0.5 - KY / 2.0
    for group in range(-(-slots // LANES)):
        start = group * LANES
        stop = min(slots, start + LANES)

        def gather(s, carry):
            values, params = carry
            turbine = jnp.maximum(slot_turbine[s], 0)
            first_x = jnp.minimum(corner[0, s], count - KX)
            first_y = jnp.minimum(corner[1, s], width - KY)
            first_z = jnp.minimum(corner[2, s], depth - KZ)
            block = conv[pl.ds(first_x, KX), pl.ds(first_y, KY)].reshape(KX * KY, depth)
            block = pltpu.roll(block, lax.rem(s - start - first_z + depth, depth), 1)
            mine = lane == s - start
            values = jnp.where(wide == s - start, block, values)
            base = lax.div(turbine, turb_dev) * (5 * turb_dev) + lax.rem(turbine, turb_dev)
            params = tuple(
                jnp.where(mine, table[base + i * turb_dev], p) for i, p in enumerate(params)
            )
            return values, params

        zero = jnp.zeros((1, LANES), jnp.float32)
        values, (sub_x, sub_y, cosine, sine, thrust) = lax.fori_loop(
            start, stop, gather, (jnp.zeros((KX * KY, LANES), jnp.float32), (zero,) * 5), unroll=2
        )
        delta_x, delta_y = cell_x - sub_x, cell_y - sub_y
        along = cosine * delta_x + sine * delta_y
        across = cosine * delta_y - sine * delta_x
        kernel = thrust * jnp.exp(
            -along * along / (2.0 * SIGMA_AXIAL * SIGMA_AXIAL)
            - across * across / (2.0 * SIGMA_RADIAL * SIGMA_RADIAL)
        )
        weighted = kernel * values
        axial = along * (1.0 / (SIGMA_AXIAL * SIGMA_AXIAL))
        radial = across * (1.0 / (SIGMA_RADIAL * SIGMA_RADIAL))
        part = pl.ds(start, LANES)
        slopes[0:1, part] = jnp.sum(
            weighted * (axial * cosine - radial * sine), axis=0, keepdims=True
        )
        slopes[1:2, part] = jnp.sum(
            weighted * (axial * sine + radial * cosine), axis=0, keepdims=True
        )
    for i in range(chunks):
        chunk_out(i).wait()


def slot_slopes(state, slot_turbine, slot_corner, table, turb_dev):
    _, count, width, depth = state.shape
    padded = -(-slot_turbine.shape[0] // LANES) * LANES
    smem = pl.BlockSpec(memory_space=pltpu.SMEM)
    return pl.pallas_call(
        functools.partial(slope_kernel, turb_dev),
        out_shape=(
            jax.ShapeDtypeStruct(state.shape, jnp.float32),
            jax.ShapeDtypeStruct((2, padded), jnp.float32),
        ),
        in_specs=[
            smem,
            smem,
            smem,
            pl.BlockSpec(memory_space=pl.ANY),
            pl.BlockSpec(memory_space=pltpu.VMEM),
        ],
        out_specs=(
            pl.BlockSpec(memory_space=pl.ANY),
            pl.BlockSpec(memory_space=pltpu.VMEM),
        ),
        scratch_shapes=[
            pltpu.VMEM(state.shape, jnp.float32),
            pltpu.VMEM((count, width, depth), jnp.float32),
            pltpu.SemaphoreType.DMA((count // CHUNK,)),
            pltpu.SemaphoreType.DMA((count // CHUNK,)),
        ],
        compiler_params=pltpu.CompilerParams(vmem_limit_bytes=40 * 1024 * 1024),
        name="slopes",
    )(slot_turbine, slot_corner, table, state, jnp.asarray(z_weights(depth)))


def finish_kernel(
    sizes, turb_dev, step_size, slopes, ids, moved, step_out, incoming, every, ssem, rsem
):
    n_gx, n_gy = sizes
    n = n_gx * n_gy
    gx, gy = lax.axis_index("gx"), lax.axis_index("gy")
    me = gx * n_gy + gy
    padded = slopes.shape[1]
    barrier = pltpu.get_barrier_semaphore()

    def peer(i):
        other = lax.rem(me + i, n)
        return (lax.div(other, n_gy), lax.rem(other, n_gy))

    @pl.loop(1, n)
    def _(i):
        pl.semaphore_signal(barrier, inc=1, device_id=peer(i), device_id_type=MESH)

    pl.semaphore_wait(barrier, n - 1)

    def send(i):
        return pltpu.make_async_remote_copy(
            src_ref=slopes,
            dst_ref=every.at[me],
            send_sem=ssem.at[i],
            recv_sem=rsem.at[me],
            device_id=peer(i),
            device_id_type=MESH,
        )

    @pl.loop(1, n)
    def _(i):
        send(i).start()

    every[me] = slopes[...]

    total = moved.shape[1]
    mine = (moved[0:1] == me.astype(jnp.float32)).astype(jnp.float32)
    before = lax.broadcasted_iota(jnp.int32, (total, total), 0) < lax.broadcasted_iota(
        jnp.int32, (total, total), 1
    )
    rank = jnp.dot(
        jnp.broadcast_to(mine, (RECV, total)).astype(jnp.bfloat16),
        before.astype(jnp.float32).astype(jnp.bfloat16),
        preferred_element_type=jnp.float32,
    )
    slot = lax.broadcasted_iota(jnp.int32, (RECV, total), 0).astype(jnp.float32)
    chosen = jnp.where((rank == slot) & (jnp.broadcast_to(mine, (RECV, total)) > 0), 1.0, 0.0)
    valid = jnp.sum(chosen, axis=1, keepdims=True)
    fields = [jnp.sum(chosen * moved[i : i + 1], axis=1, keepdims=True) for i in range(1, 7)]
    wanted, sub_x, sub_y, cosine, sine, thrust = fields
    own = (
        me * turb_dev + lax.broadcasted_iota(jnp.int32, (turb_dev, padded), 0)
    ).astype(jnp.float32)
    targets = jnp.concatenate([own, jnp.broadcast_to(wanted, (RECV, padded))], axis=0)

    @pl.loop(1, n)
    def _(i):
        send(i).wait_send()
        other = lax.rem(me + i, n)
        pltpu.make_async_remote_copy(
            src_ref=slopes,
            dst_ref=every.at[other],
            send_sem=ssem.at[i],
            recv_sem=rsem.at[other],
            device_id=peer(i),
            device_id_type=MESH,
        ).wait_recv()

    def collect(d, carry):
        sum_x, sum_y = carry
        hit = targets == ids[d]
        both = every[d]
        return (
            sum_x + jnp.where(hit, both[0:1], 0.0),
            sum_y + jnp.where(hit, both[1:2], 0.0),
        )

    zero = jnp.zeros((turb_dev + RECV, padded), jnp.float32)
    sums = lax.fori_loop(0, n, collect, (zero, zero), unroll=2)
    step = step_size[0]
    taken = [
        jnp.clip(-step * jnp.sum(part, axis=1, keepdims=True), -0.5, 0.5) for part in sums
    ]
    flip = lax.broadcasted_iota(jnp.int32, (turb_dev, turb_dev), 0) == lax.broadcasted_iota(
        jnp.int32, (turb_dev, turb_dev), 1
    )
    for i in range(2):
        step_out[i : i + 1] = jnp.sum(
            jnp.where(flip, taken[i][:turb_dev], 0.0), axis=0, keepdims=True
        )
    cells = KX * KY * KZ
    cell = lax.broadcasted_iota(jnp.int32, (RECV, cells), 1)
    ex = (cell // (KY * KZ)).astype(jnp.float32) + 0.5 - KX / 2.0
    ey = lax.rem(cell // KZ, KY).astype(jnp.float32) + 0.5 - KY / 2.0
    ez = lax.rem(cell, KZ).astype(jnp.float32) + 0.5 - KZ / 2.0
    delta_x = ex - (sub_x + taken[0][turb_dev:])
    delta_y = ey - (sub_y + taken[1][turb_dev:])
    along = cosine * delta_x + sine * delta_y
    across = cosine * delta_y - sine * delta_x
    kernel = thrust * jnp.exp(
        -along * along / (2.0 * SIGMA_AXIAL * SIGMA_AXIAL)
        - (across * across + ez * ez) / (2.0 * SIGMA_RADIAL * SIGMA_RADIAL)
    )
    incoming[...] = jnp.where(valid > 0, kernel, 0.0).astype(jnp.bfloat16)


def finish(step_size, slopes, ids, moved, turb_dev, sizes):
    n = sizes[0] * sizes[1]
    vmem = pl.BlockSpec(memory_space=pltpu.VMEM)

    def kernel(step_ref, slopes_ref, ids_ref, moved_ref, *rest):
        finish_kernel(sizes, turb_dev, step_ref, slopes_ref, ids_ref, moved_ref, *rest)

    return pl.pallas_call(
        kernel,
        out_shape=(
            jax.ShapeDtypeStruct((2, turb_dev), jnp.float32),
            jax.ShapeDtypeStruct((RECV, KX * KY * KZ), jnp.bfloat16),
        ),
        in_specs=[pl.BlockSpec(memory_space=pltpu.SMEM), vmem, vmem, vmem],
        out_specs=(vmem, vmem),
        scratch_shapes=[
            pltpu.VMEM((n,) + slopes.shape, jnp.float32),
            pltpu.SemaphoreType.DMA((n,)),
            pltpu.SemaphoreType.DMA((n,)),
        ],
        compiler_params=pltpu.CompilerParams(collective_id=1, has_side_effects=True),
        name="finish",
    )(step_size, slopes, ids, moved)


def body(
    sizes, adjoint, medium, rotors, step_size, slot_turbine, slot_corner, moved_rotors, new_brick
):
    turb_dev = rotors.shape[1]
    slots = slot_turbine.shape[0]
    padded = -(-slots // LANES) * LANES
    moved_dev = moved_rotors.shape[0]
    brick = lax.axis_index("gx") * sizes[1] + lax.axis_index("gy")
    full = jnp.stack([rotors[0], rotors[1], jnp.cos(rotors[2]), jnp.sin(rotors[2]), rotors[3]])
    picked = (moved_rotors[:, None] == jnp.arange(turb_dev)[None, :])[None]
    picked = jnp.sum(jnp.where(picked, full[:, None, :], 0.0), axis=2)
    fields = jnp.concatenate(
        [
            new_brick[:, 0].astype(jnp.float32)[None],
            (brick * turb_dev + moved_rotors).astype(jnp.float32)[None],
            picked,
        ]
    )
    ids = jnp.pad(slot_turbine.astype(jnp.float32), (0, padded - slots), constant_values=-1.0)
    packed = jnp.concatenate([full.reshape(-1), ids, fields.reshape(-1)])
    packed = jnp.pad(packed, (0, -packed.shape[0] % LANES))
    every = lax.all_gather(packed, ("gx", "gy"), axis=0)
    n = every.shape[0]
    cut = 5 * turb_dev
    table = every[:, :cut].reshape(-1)
    every_ids = every[:, None, cut : cut + padded]
    every_moved = every[:, cut + padded : cut + padded + 7 * moved_dev]
    every_moved = every_moved.reshape(n, 7, moved_dev).transpose(1, 0, 2).reshape(7, n * moved_dev)

    state = relax(adjoint, medium, sizes)
    state, slopes = slot_slopes(state, slot_turbine, slot_corner, table, turb_dev)
    step_taken, incoming = finish(
        step_size.reshape(1), slopes, every_ids, every_moved, turb_dev, sizes
    )
    return (state, step_taken, incoming)


def solution(mesh):
    sizes = (mesh.shape["gx"], mesh.shape["gy"])
    return jax.shard_map(
        functools.partial(body, sizes),
        mesh=mesh,
        in_specs=(
            P(None, "gx", "gy", None),
            P(None, "gx", "gy", None),
            P(None, ("gx", "gy")),
            P(),
            P(("gx", "gy")),
            P(None, ("gx", "gy")),
            P(("gx", "gy")),
            P(("gx", "gy"), None),
        ),
        out_specs=(P(None, "gx", "gy", None), P(None, ("gx", "gy")), P(("gx", "gy"), None)),
        check_vma=False,
    )
```

profile of v0, /device:TPU:0, one launch (start us, length us, event | category | flops | bytes accessed | tf_op | source)
XLA Modules:
  0.0 131.6 jit_solution(17335420894349578530)
XLA Ops:
  1.3 0.7 convert_bitcast_fusion
  1.9 0.7 convert_bitcast_fusion.1
  2.6 0.7 iota_compare_fusion.2
  3.3 0.7 slice.21
  4.0 0.7 convert_element_type.21
  4.7 0.8 slice_cosine_fusion
  5.5 0.1 reshape.54
  5.6 0.1 select_reduce_fusion
  5.7 0.1 reshape.55
  5.8 0.1 fusion
  5.9 70.1 %all-gather.1 = f32[32,1,640]{2,1,0:T(1,128)S(1)} all-gather(f32[1,1,640]{2,1,0:T(1,128)S(1)} %reshape.61), channel_id=2, replica_groups=mesh['gx'=4,'gy'=8] {'gx','gy'}, dimensions={0}, use_global_device_ids=true | all-gather | bytes 84480 | tf_op jit(solution)/shard_map/all_gather | solution.py:513
  76.0 0.1 slice.29
  76.0 0.1 copy.17
  76.1 0.1 slice.28
  76.2 0.1 reshape.56.table
  76.3 0.6 broadcast_in_dim.35.ids_ref
  77.0 0.1 copy.18
  77.1 0.7 reshape.59.moved_ref
  77.8 0.0 copy-start.1
  77.8 0.0 copy-start.2
  77.8 0.0 copy-start.3
  77.8 22.3 %relax.1.q_hbm = f32[2,64,96,128]{3,2,1,0:T(8,128)} custom-call(f32[2,64,96,128]{3,2,1,0:T(8,128)} %q_hbm.1, bf16[5,64,96,128]{3,2,1,0:T(8,128)(2,1)} %med_hbm.1), custom_call_target="tpu_custom_call" | custom-call | tf_op jit(solution)/shard_map/relax/pallas_call | solution.py:209
  100.1 0.0 copy-done.1
  100.2 0.0 copy-done.2
  100.2 0.0 copy-done.3
  100.2 0.0 copy-start
  100.2 2.8 %copy-done = f32[2,64,96,128]{3,2,1,0:T(8,128)S(1)} copy-done((f32[2,64,96,128]{3,2,1,0:T(8,128)S(1)}, f32[2,64,96,128]{3,2,1,0:T(8,128)}, u32[]{:S(2)}) %copy-start) | copy-done | bytes 6291480
  103.0 15.3 %slopes.1 = (f32[2,64,96,128]{3,2,1,0:T(8,128)}, f32[2,256]{1,0:T(2,128)S(1)}) custom-call(s32[192]{0:T(256)S(1)} %copy-done.3, s32[3,192]{1,0:T(4,128)S(1)} %copy-done.2, f32[10240]{0:T(1024)S(1)} %reshape.56.table, f32[2,64,96,128]{3,2,1,0:T(8,128)S(1)} %copy-done, bf16[256,256]{1,0:T(8,128)(2,1)S(1)} %copy-done.1), custom_call_target="tpu_custom_call" | custom-call | tf_op jit(solution)/shard_map/slopes/pallas_call | solution.py:332
  118.2 0.0 copy-start.4
  118.3 0.6 copy-done.4
  118.8 10.2 %finish.1 = (f32[2,64]{1,0:T(2,128)}, bf16[8,2048]{1,0:T(8,128)(2,1)}) custom-call(f32[1]{0:T(128)} %bitcast.11.step_ref, f32[2,256]{1,0:T(2,128)} %copy-done.4, f32[32,1,256]{2,1,0:T(1,128)} %broadcast_in_dim.35.ids_ref, f32[7,128]{1,0:T(8,128)} %reshape.59.moved_ref), custom_call_target="tpu_custom_call" | custom-call | tf_op jit(solution)/shard_map/finish/pallas_call | solution.py:474
  129.0 1.2 copy.25
  130.3 1.4 %copy.26 = bf16[8,2048]{1,0:T(8,128)(2,1)} copy(bf16[8,2048]{1,0:T(8,128)(2,1)} %get-tuple-element.19) | data formatting | bytes 65536
  (7 shorter events, 0.1 us)
Async XLA Ops:
  77.8 22.4 %copy-start.1 = (bf16[256,256]{1,0:T(8,128)(2,1)S(1)}, bf16[256,256]{1,0:T(8,128)(2,1)}, u32[]{:S(2)}) copy-start(bf16[256,256]{1,0:T(8,128)(2,1)} %constant.20.clone.profile) | copy-start | bytes 393220
  77.8 22.4 %copy-start.2 = (s32[3,192]{1,0:T(4,128)S(1)}, s32[3,192]{1,0:T(4,128)}, u32[]{:S(2)}) copy-start(s32[3,192]{1,0:T(4,128)} %corner.1) | copy-start | bytes 6916
  77.8 22.4 %copy-start.3 = (s32[192]{0:T(256)S(1)}, s32[192]{0:T(256)}, u32[]{:S(2)}) copy-start(s32[192]{0:T(256)} %slot_turbine.1) | copy-start | bytes 2308
  100.2 2.8 %copy-start = (f32[2,64,96,128]{3,2,1,0:T(8,128)S(1)}, f32[2,64,96,128]{3,2,1,0:T(8,128)}, u32[]{:S(2)}) copy-start(f32[2,64,96,128]{3,2,1,0:T(8,128)} %relax.1.q_hbm) | copy-start | bytes 18874372
  118.2 0.6 copy-start.4
where the time goes:
time: 132 us
  blocking collectives  70.1 us (53%)
  Pallas kernels  47.8 us (36%)
  local copies, waits for them, and re-layouts  9.43 us (7%)
  other arithmetic  2.91 us (2%)
  between operations  1.38 us (1%)
    all_gather x1, blocking collectives, body(): every = lax.all_gather(packed, ('gx', 'gy'), axis=0)  70.1 us
    pallas_call x1, Pallas kernels, relax(): pl.pallas_call(functools.partial(relax_kernel, sizes), out_shape=jax.Shap...  22.3 us
    pallas_call x1, Pallas kernels, slot_slopes(): pl.pallas_call(functools.partial(slope_kernel, turb_dev), out_shape=(jax....  15.3 us
    pallas_call x1, Pallas kernels, finish(): pl.pallas_call(kernel, out_shape=(jax.ShapeDtypeStruct((2, turb_dev), jnp...  10.2 us
    unnamed x14, local copies, waits for them, and re-layouts  5.98 us

commit v1 on v0

--- a/solution.py
+++ b/solution.py
@@ -52,10 +52,66 @@
     dst[1, x] = e + TAU * (sides[1] - (diagonal + reaction) * e - coupling * k)
 
 
+def pack_tables(me, rotors, listed, moved, target, pack):
+    turb_dev, slots, moved_dev = rotors.shape[1], listed.shape[1], moved.shape[0]
+    pack[...] = jnp.full(pack.shape, -1.0, jnp.float32)
+    own = pl.ds(0, turb_dev)
+    pack[0:2, own] = rotors[0:2]
+    pack[2:3, own] = jnp.cos(rotors[2:3])
+    pack[3:4, own] = jnp.sin(rotors[2:3])
+    pack[4:5, own] = rotors[3:4]
+    for group in range(-(-slots // LANES)):
+        size = min(LANES, slots - group * LANES)
+        pack[5 + group : 6 + group, pl.ds(0, size)] = listed[
+            :, pl.ds(group * LANES, size)
+        ].astype(jnp.float32)
+    full = pack[...]
+    lane = lax.broadcasted_iota(jnp.int32, full.shape, 1)
+    field = lax.broadcasted_iota(jnp.int32, full.shape, 0) + 2
+    line = jnp.full((1, LANES), -1.0, jnp.float32)
+    for j in range(moved_dev):
+        picked = jnp.sum(jnp.where(lane == moved[j], full, 0.0), axis=1, keepdims=True)
+        here = (lane == moved_dev * field + j) & (field < 7)
+        spread = jnp.sum(jnp.where(here, picked, 0.0), axis=0, keepdims=True)
+        place = lane[0:1]
+        for f in range(2, 7):
+            line = jnp.where(place == moved_dev * f + j, spread, line)
+        line = jnp.where(place == j, target[j, 0].astype(jnp.float32), line)
+        number = (me * turb_dev + moved[j]).astype(jnp.float32)
+        line = jnp.where(place == moved_dev + j, number, line)
+    pack[7:8] = line
+
+
 def relax_kernel(
-    sizes, q_hbm, med_hbm, out_hbm, q, med, q1, prev, xs, xr, ys, yr, edge_sem, in_sem, out_sem, ssem, rsem
+    sizes,
+    rotors,
+    listed,
+    moved,
+    target,
+    q_hbm,
+    med_hbm,
+    out_hbm,
+    every,
+    q,
+    med,
+    q1,
+    prev,
+    xs,
+    xr,
+    ys,
+    yr,
+    pack,
+    table,
+    edge_sem,
+    in_sem,
+    out_sem,
+    ssem,
+    rsem,
+    tsend,
+    trecv,
 ):
     n_gx, n_gy = sizes
+    n = n_gx * n_gy
     _, count, width, _ = q.shape
     chunks = count // CHUNK
     gx, gy = lax.axis_index("gx"), lax.axis_index("gy")
@@ -89,9 +145,31 @@
             copy.start()
 
     barrier = pltpu.get_barrier_semaphore()
-    for peer in peers:
-        pl.semaphore_signal(barrier, inc=1, device_id=peer, device_id_type=MESH)
-    pl.semaphore_wait(barrier, 4)
+    me = gx * n_gy + gy
+
+    @pl.loop(1, n)
+    def _(i):
+        other = lax.rem(me + i, n)
+        pl.semaphore_signal(
+            barrier,
+            inc=1,
+            device_id=(lax.div(other, n_gy), lax.rem(other, n_gy)),
+            device_id_type=MESH,
+        )
+
+    pack_tables(me, rotors, listed, moved, target, pack)
+    pl.semaphore_wait(barrier, n - 1)
+
+    def share(i, place):
+        other = lax.rem(me + i, n)
+        return pltpu.make_async_remote_copy(
+            src_ref=pack,
+            dst_ref=table.at[place],
+            send_sem=tsend.at[i],
+            recv_sem=trecv.at[place],
+            device_id=(lax.div(other, n_gy), lax.rem(other, n_gy)),
+            device_id_type=MESH,
+        )
 
     def exchange(turn, src):
         for c in range(2):
@@ -159,6 +237,12 @@
             copy.wait()
 
     copies = exchange(0, q)
+
+    @pl.loop(1, n)
+    def _(i):
+        share(i, me).start()
+
+    table[me] = pack[...]
     prev[...] = jnp.zeros_like(prev)
     for i in range(chunks):
         if 0 < i + 1 < chunks - 1:
@@ -191,6 +275,12 @@
             outs.append(chunk_out(i))
             outs[-1].start()
 
+    @pl.loop(1, n)
+    def _(i):
+        share(i, me).wait_send()
+        share(i, lax.rem(me + i, n)).wait_recv()
+
+    every[...] = table[...]
     for copy in copies:
         copy.wait()
     patch(1, q)
@@ -204,13 +294,18 @@
         copy.wait()
 
 
-def relax(adjoint, medium, sizes):
+def relax(adjoint, medium, rotors, slot_turbine, moved_rotors, new_brick, sizes):
+    n = sizes[0] * sizes[1]
+    vmem, smem = pl.BlockSpec(memory_space=pltpu.VMEM), pl.BlockSpec(memory_space=pltpu.SMEM)
     channels, count, width, depth = adjoint.shape
     return pl.pallas_call(
         functools.partial(relax_kernel, sizes),
-        out_shape=jax.ShapeDtypeStruct(adjoint.shape, jnp.float32),
-        in_specs=[pl.BlockSpec(memory_space=pl.ANY)] * 2,
-        out_specs=pl.BlockSpec(memory_space=pl.ANY),
+        out_shape=(
+            jax.ShapeDtypeStruct(adjoint.shape, jnp.float32),
+            jax.ShapeDtypeStruct((n, 8, LANES), jnp.float32),
+        ),
+        in_specs=[vmem, vmem, smem, smem] + [pl.BlockSpec(memory_space=pl.ANY)] * 2,
+        out_specs=(pl.BlockSpec(memory_space=pl.ANY), vmem),
         scratch_shapes=[
             pltpu.VMEM(adjoint.shape, jnp.float32),
             pltpu.VMEM(medium.shape, jnp.bfloat16),
@@ -220,17 +315,21 @@
             pltpu.VMEM((2, 2, channels, width, depth), jnp.float32),
             pltpu.VMEM((2, 2, channels, count, depth), jnp.float32),
             pltpu.VMEM((2, 2, channels, count, depth), jnp.float32),
+            pltpu.VMEM((8, LANES), jnp.float32),
+            pltpu.VMEM((n, 8, LANES), jnp.float32),
             pltpu.SemaphoreType.DMA((2, 2)),
             pltpu.SemaphoreType.DMA((count // CHUNK, 3)),
             pltpu.SemaphoreType.DMA((2 + count // CHUNK,)),
             pltpu.SemaphoreType.DMA((2, 4)),
             pltpu.SemaphoreType.DMA((2, 4)),
+            pltpu.SemaphoreType.DMA((n,)),
+            pltpu.SemaphoreType.DMA((n,)),
         ],
         compiler_params=pltpu.CompilerParams(
             collective_id=0, has_side_effects=True, vmem_limit_bytes=48 * 1024 * 1024
         ),
         name="relax",
-    )(adjoint, medium)
+    )(rotors, slot_turbine[None, :], moved_rotors, new_brick, adjoint, medium)
 
 
 def z_weights(depth):
@@ -244,7 +343,20 @@
 
 
 def slope_kernel(
-    turb_dev, slot_turbine, corner, table, q_hbm, profile, out_hbm, slopes, q, conv, in_sem, out_sem
+    turb_dev,
+    slot_turbine,
+    corner,
+    table_hbm,
+    q_hbm,
+    profile,
+    out_hbm,
+    slopes,
+    q,
+    conv,
+    table,
+    table_sem,
+    in_sem,
+    out_sem,
 ):
     _, count, width, depth = q.shape
     chunks = count // CHUNK
@@ -258,6 +370,8 @@
         part = pl.ds(i * CHUNK, CHUNK)
         return pltpu.make_async_copy(q.at[:, part], out_hbm.at[:, part], out_sem.at[i])
 
+    fetch = pltpu.make_async_copy(table_hbm, table, table_sem)
+    fetch.start()
     for i in range(chunks):
         chunk_in(i).start()
     for i in range(chunks):
@@ -275,12 +389,15 @@
             CHUNK, width, depth
         )
 
+    fetch.wait()
+    slopes[...] = jnp.zeros_like(slopes)
+    groups = -(-slots // LANES)
     lane = lax.broadcasted_iota(jnp.int32, (1, LANES), 1)
     wide = lax.broadcasted_iota(jnp.int32, (KX * KY, LANES), 1)
     cell = lax.broadcasted_iota(jnp.int32, (KX * KY, LANES), 0)
     cell_x = (cell // KY).astype(jnp.float32) + 0.5 - KX / 2.0
     cell_y = lax.rem(cell, KY).astype(jnp.float32) + 0.5 - KY / 2.0
-    for group in range(-(-slots // LANES)):
+    for group in range(groups):
         start = group * LANES
         stop = min(slots, start + LANES)
 
@@ -294,9 +411,9 @@
             block = pltpu.roll(block, lax.rem(s - start - first_z + depth, depth), 1)
             mine = lane == s - start
             values = jnp.where(wide == s - start, block, values)
-            base = lax.div(turbine, turb_dev) * (5 * turb_dev) + lax.rem(turbine, turb_dev)
+            owner, local = lax.div(turbine, turb_dev), lax.rem(turbine, turb_dev)
             params = tuple(
-                jnp.where(mine, table[base + i * turb_dev], p) for i, p in enumerate(params)
+                jnp.where(mine, table[owner, i, local], p) for i, p in enumerate(params)
             )
             return values, params
 
@@ -314,11 +431,11 @@
         weighted = kernel * values
         axial = along * (1.0 / (SIGMA_AXIAL * SIGMA_AXIAL))
         radial = across * (1.0 / (SIGMA_RADIAL * SIGMA_RADIAL))
-        part = pl.ds(start, LANES)
-        slopes[0:1, part] = jnp.sum(
+        other = groups + group
+        slopes[group : group + 1] = jnp.sum(
             weighted * (axial * cosine - radial * sine), axis=0, keepdims=True
         )
-        slopes[1:2, part] = jnp.sum(
+        slopes[other : other + 1] = jnp.sum(
             weighted * (axial * sine + radial * cosine), axis=0, keepdims=True
         )
     for i in range(chunks):
@@ -327,18 +444,17 @@
 
 def slot_slopes(state, slot_turbine, slot_corner, table, turb_dev):
     _, count, width, depth = state.shape
-    padded = -(-slot_turbine.shape[0] // LANES) * LANES
     smem = pl.BlockSpec(memory_space=pltpu.SMEM)
     return pl.pallas_call(
         functools.partial(slope_kernel, turb_dev),
         out_shape=(
             jax.ShapeDtypeStruct(state.shape, jnp.float32),
-            jax.ShapeDtypeStruct((2, padded), jnp.float32),
+            jax.ShapeDtypeStruct((8, LANES), jnp.float32),
         ),
         in_specs=[
             smem,
             smem,
-            smem,
+            pl.BlockSpec(memory_space=pl.ANY),
             pl.BlockSpec(memory_space=pl.ANY),
             pl.BlockSpec(memory_space=pltpu.VMEM),
         ],
@@ -349,22 +465,24 @@
         scratch_shapes=[
             pltpu.VMEM(state.shape, jnp.float32),
             pltpu.VMEM((count, width, depth), jnp.float32),
+            pltpu.SMEM(table.shape, jnp.float32),
+            pltpu.SemaphoreType.DMA,
             pltpu.SemaphoreType.DMA((count // CHUNK,)),
             pltpu.SemaphoreType.DMA((count // CHUNK,)),
         ],
-        compiler_params=pltpu.CompilerParams(vmem_limit_bytes=40 * 1024 * 1024),
+        compiler_params=pltpu.CompilerParams(vmem_limit_bytes=58 * 1024 * 1024),
         name="slopes",
     )(slot_turbine, slot_corner, table, state, jnp.asarray(z_weights(depth)))
 
 
 def finish_kernel(
-    sizes, turb_dev, step_size, slopes, ids, moved, step_out, incoming, every, ssem, rsem
+    sizes, groups, moved_dev, step_size, slopes, table, step_out, incoming, every, ssem, rsem
 ):
     n_gx, n_gy = sizes
     n = n_gx * n_gy
     gx, gy = lax.axis_index("gx"), lax.axis_index("gy")
     me = gx * n_gy + gy
-    padded = slopes.shape[1]
+    turb_dev = step_out.shape[1]
     barrier = pltpu.get_barrier_semaphore()
 
     def peer(i):
@@ -393,25 +511,38 @@
 
     every[me] = slopes[...]
 
-    total = moved.shape[1]
-    mine = (moved[0:1] == me.astype(jnp.float32)).astype(jnp.float32)
-    before = lax.broadcasted_iota(jnp.int32, (total, total), 0) < lax.broadcasted_iota(
-        jnp.int32, (total, total), 1
+    lines = table[:, 7]
+    lane = lax.broadcasted_iota(jnp.int32, lines.shape, 1)
+    mine = jnp.where((lines == me.astype(jnp.float32)) & (lane < moved_dev), 1.0, 0.0)
+
+    def earlier(size, row, col):
+        less = lax.broadcasted_iota(jnp.int32, (size, size), row) < lax.broadcasted_iota(
+            jnp.int32, (size, size), col
+        )
+        return jnp.where(less, 1.0, 0.0).astype(jnp.bfloat16)
+
+    rank = jnp.sum(
+        jnp.dot(
+            earlier(n, 1, 0), mine.astype(jnp.bfloat16), preferred_element_type=jnp.float32
+        ),
+        axis=1,
+        keepdims=True,
+    ) + jnp.dot(
+        mine.astype(jnp.bfloat16), earlier(LANES, 0, 1), preferred_element_type=jnp.float32
     )
-    rank = jnp.dot(
-        jnp.broadcast_to(mine, (RECV, total)).astype(jnp.bfloat16),
-        before.astype(jnp.float32).astype(jnp.bfloat16),
-        preferred_element_type=jnp.float32,
-    )
-    slot = lax.broadcasted_iota(jnp.int32, (RECV, total), 0).astype(jnp.float32)
-    chosen = jnp.where((rank == slot) & (jnp.broadcast_to(mine, (RECV, total)) > 0), 1.0, 0.0)
-    valid = jnp.sum(chosen, axis=1, keepdims=True)
-    fields = [jnp.sum(chosen * moved[i : i + 1], axis=1, keepdims=True) for i in range(1, 7)]
-    wanted, sub_x, sub_y, cosine, sine, thrust = fields
+    shifted = [pltpu.roll(lines, LANES - moved_dev * f, 1) for f in range(1, 7)]
+    chosen = [jnp.where(rank == float(slot), mine, 0.0) for slot in range(RECV)]
+
+    def per_slot(values):
+        parts = [jnp.sum(pick * values, axis=0, keepdims=True) for pick in chosen]
+        return jnp.sum(jnp.concatenate(parts, axis=0), axis=1, keepdims=True)
+
+    valid = per_slot(jnp.ones_like(lines))
+    wanted, sub_x, sub_y, cosine, sine, thrust = [per_slot(values) for values in shifted]
     own = (
-        me * turb_dev + lax.broadcasted_iota(jnp.int32, (turb_dev, padded), 0)
+        me * turb_dev + lax.broadcasted_iota(jnp.int32, (turb_dev, LANES), 0)
     ).astype(jnp.float32)
-    targets = jnp.concatenate([own, jnp.broadcast_to(wanted, (RECV, padded))], axis=0)
+    targets = jnp.concatenate([own, jnp.broadcast_to(wanted, (RECV, LANES))], axis=0)
 
     @pl.loop(1, n)
     def _(i):
@@ -428,14 +559,13 @@
 
     def collect(d, carry):
         sum_x, sum_y = carry
-        hit = targets == ids[d]
-        both = every[d]
-        return (
-            sum_x + jnp.where(hit, both[0:1], 0.0),
-            sum_y + jnp.where(hit, both[1:2], 0.0),
-        )
-
-    zero = jnp.zeros((turb_dev + RECV, padded), jnp.float32)
+        for group in range(groups):
+            hit = targets == table[d, pl.ds(5 + group, 1)]
+            sum_x = sum_x + jnp.where(hit, every[d, pl.ds(group, 1)], 0.0)
+            sum_y = sum_y + jnp.where(hit, every[d, pl.ds(groups + group, 1)], 0.0)
+        return sum_x, sum_y
+
+    zero = jnp.zeros((turb_dev + RECV, LANES), jnp.float32)
     sums = lax.fori_loop(0, n, collect, (zero, zero), unroll=2)
     step = step_size[0]
     taken = [
@@ -464,20 +594,17 @@
     incoming[...] = jnp.where(valid > 0, kernel, 0.0).astype(jnp.bfloat16)
 
 
-def finish(step_size, slopes, ids, moved, turb_dev, sizes):
+def finish(step_size, slopes, table, turb_dev, groups, moved_dev, sizes):
     n = sizes[0] * sizes[1]
     vmem = pl.BlockSpec(memory_space=pltpu.VMEM)
 
-    def kernel(step_ref, slopes_ref, ids_ref, moved_ref, *rest):
-        finish_kernel(sizes, turb_dev, step_ref, slopes_ref, ids_ref, moved_ref, *rest)
-
     return pl.pallas_call(
-        kernel,
+        functools.partial(finish_kernel, sizes, groups, moved_dev),
         out_shape=(
             jax.ShapeDtypeStruct((2, turb_dev), jnp.float32),
             jax.ShapeDtypeStruct((RECV, KX * KY * KZ), jnp.bfloat16),
         ),
-        in_specs=[pl.BlockSpec(memory_space=pltpu.SMEM), vmem, vmem, vmem],
+        in_specs=[pl.BlockSpec(memory_space=pltpu.SMEM), vmem, vmem],
         out_specs=(vmem, vmem),
         scratch_shapes=[
             pltpu.VMEM((n,) + slopes.shape, jnp.float32),
@@ -486,42 +613,18 @@
         ],
         compiler_params=pltpu.CompilerParams(collective_id=1, has_side_effects=True),
         name="finish",
-    )(step_size, slopes, ids, moved)
+    )(step_size, slopes, table)
 
 
 def body(
     sizes, adjoint, medium, rotors, step_size, slot_turbine, slot_corner, moved_rotors, new_brick
 ):
     turb_dev = rotors.shape[1]
-    slots = slot_turbine.shape[0]
-    padded = -(-slots // LANES) * LANES
-    moved_dev = moved_rotors.shape[0]
-    brick = lax.axis_index("gx") * sizes[1] + lax.axis_index("gy")
-    full = jnp.stack([rotors[0], rotors[1], jnp.cos(rotors[2]), jnp.sin(rotors[2]), rotors[3]])
-    picked = (moved_rotors[:, None] == jnp.arange(turb_dev)[None, :])[None]
-    picked = jnp.sum(jnp.where(picked, full[:, None, :], 0.0), axis=2)
-    fields = jnp.concatenate(
-        [
-            new_brick[:, 0].astype(jnp.float32)[None],
-            (brick * turb_dev + moved_rotors).astype(jnp.float32)[None],
-            picked,
-        ]
-    )
-    ids = jnp.pad(slot_turbine.astype(jnp.float32), (0, padded - slots), constant_values=-1.0)
-    packed = jnp.concatenate([full.reshape(-1), ids, fields.reshape(-1)])
-    packed = jnp.pad(packed, (0, -packed.shape[0] % LANES))
-    every = lax.all_gather(packed, ("gx", "gy"), axis=0)
-    n = every.shape[0]
-    cut = 5 * turb_dev
-    table = every[:, :cut].reshape(-1)
-    every_ids = every[:, None, cut : cut + padded]
-    every_moved = every[:, cut + padded : cut + padded + 7 * moved_dev]
-    every_moved = every_moved.reshape(n, 7, moved_dev).transpose(1, 0, 2).reshape(7, n * moved_dev)
-
-    state = relax(adjoint, medium, sizes)
+    groups = -(-slot_turbine.shape[0] // LANES)
+    state, table = relax(adjoint, medium, rotors, slot_turbine, moved_rotors, new_brick, sizes)
     state, slopes = slot_slopes(state, slot_turbine, slot_corner, table, turb_dev)
     step_taken, incoming = finish(
-        step_size.reshape(1), slopes, every_ids, every_moved, turb_dev, sizes
+        step_size.reshape(1), slopes, table, turb_dev, groups, moved_rotors.shape[0], sizes
     )
     return (state, step_taken, incoming)
 

time: 132 us -> 64.2 us (0.49)
  blocking collectives: 70.1 us -> 0 us
  Pallas kernels: 47.8 us -> 56.6 us
  local copies, waits for them, and re-layouts: 9.43 us -> 6.01 us
  other arithmetic: 2.91 us -> 0 us
    all_gather x1 -> x0, blocking collectives: 70.1 us -> none  [body(): every = lax.all_gather(packed, ('gx', 'gy'), axis=0)]
    pallas_call x2, Pallas kernels: 32.5 us -> 39.4 us  [the longest x1 28.5 us: relax(): pl.pallas_call(functools.partial(relax_kernel, sizes), out_shape=(jax.Sha...]
    pallas_call x1, Pallas kernels: 15.3 us -> 17.2 us  [slot_slopes(): pl.pallas_call(functools.partial(slope_kernel, turb_dev), out_shape=(jax....]
    convert_element_type x2 -> x0, other arithmetic: 1.34 us -> none  [the longest x1 0.68 us: body(): slot_turbine.astype(jnp.float32)]
    unnamed x14 -> x11, local copies, waits for them, and re-layouts: 5.98 us -> 6.01 us
where the time goes in v1:
time: 64.2 us; the launch traced here: 63.9 us
  Pallas kernels  56.6 us (88%)
  local copies, waits for them, and re-layouts  6.01 us (9%)
  between operations  1.31 us (2%)
    pallas_call x1, Pallas kernels, relax(): pl.pallas_call(functools.partial(relax_kernel, sizes), out_shape=(jax.Sha...  28.5 us
    pallas_call x1, Pallas kernels, slot_slopes(): pl.pallas_call(functools.partial(slope_kernel, turb_dev), out_shape=(jax....  17.2 us
    pallas_call x1, Pallas kernels, finish(): pl.pallas_call(functools.partial(finish_kernel, sizes, groups, moved_dev)...  10.9 us
    unnamed x11, local copies, waits for them, and re-layouts  6.01 us

profile of v1, /device:TPU:0, one launch (start us, length us, event | category | flops | bytes accessed | tf_op | source)
XLA Modules:
  0.0 63.9 jit_solution(11726910686942913166)
XLA Ops:
  0.6 0.7 %copy.12.target = s32[4,1]{1,0:T(4,128)S(1)} copy(s32[4,1]{0,1:T(1,128)} %param.16) | data formatting | bytes 32 | tf_op args[7]
  1.4 0.0 copy-start.1
  1.4 0.7 %copy-done.1 = s32[192]{0:T(256)S(1)} copy-done((s32[192]{0:T(256)S(1)}, s32[192]{0:T(256)}, u32[]{:S(2)}) %copy-start.1) | copy-done | bytes 792
  2.1 0.0 copy-start.2
  2.1 0.7 %copy-done.2 = f32[4,64]{1,0:T(4,128)S(1)} copy-done((f32[4,64]{1,0:T(4,128)S(1)}, f32[4,64]{1,0:T(4,128)}, u32[]{:S(2)}) %copy-start.2) | copy-done | bytes 1048
  2.7 0.0 copy-start.3
  2.7 0.7 %copy-done.3 = s32[4]{0:T(128)S(1)} copy-done((s32[4]{0:T(128)S(1)}, s32[4]{0:T(128)}, u32[]{:S(2)}) %copy-start.3) | copy-done | bytes 40
  3.4 28.5 %relax.1 = (f32[2,64,96,128]{3,2,1,0:T(8,128)}, f32[32,8,128]{2,1,0:T(8,128)S(1)}) custom-call(f32[4,64]{1,0:T(4,128)S(1)} %copy-done.2, s32[1,192]{1,0:T(1,128)S(1)} %bitcast.3, s32[4]{0:T(128)S(1)} %copy-done.3, s32[4,1]{1,0:T(4,128)S(1)} %copy.12.target, f32[2,64,96,128]{3,2,1,0:T(8,128)} %q_hbm.1, bf16[5,64,96,128]{3,2,1,0:T(8,128)(2,1)} %med_hbm.1), custom_call_target="tpu_custom_call" | custom-call | tf_op jit(solution)/shard_map/relax/pallas_call | solution.py:301
  31.9 0.0 copy-start
  31.9 0.7 %copy-done = f32[32,8,128]{2,1,0:T(8,128)} copy-done((f32[32,8,128]{2,1,0:T(8,128)}, f32[32,8,128]{2,1,0:T(8,128)S(1)}, u32[]{:S(2)}) %copy-start) | copy-done | bytes 131096
  32.6 17.2 %slopes.1 = (f32[2,64,96,128]{3,2,1,0:T(8,128)}, f32[8,128]{1,0:T(8,128)}) custom-call(s32[192]{0:T(256)} %slot_turbine.1, s32[3,192]{1,0:T(4,128)} %corner.1, f32[32,8,128]{2,1,0:T(8,128)} %copy-done, f32[2,64,96,128]{3,2,1,0:T(8,128)} %get-tuple-element.10.q_hbm, bf16[256,256]{1,0:T(8,128)(2,1)} %constant.2.clone.profile), custom_call_target="tpu_custom_call" | custom-call | tf_op jit(solution)/shard_map/slopes/pallas_call | solution.py:448
  50.4 10.9 %finish.1 = (f32[2,64]{1,0:T(2,128)}, bf16[8,2048]{1,0:T(8,128)(2,1)}) custom-call(f32[1]{0:T(128)} %bitcast.2.step_size, f32[8,128]{1,0:T(8,128)} %get-tuple-element.12.slopes, f32[32,8,128]{2,1,0:T(8,128)} %copy-done), custom_call_target="tpu_custom_call" | custom-call | tf_op jit(solution)/shard_map/finish/pallas_call | solution.py:601
  61.3 1.2 %copy.16 = f32[2,64]{1,0:T(2,128)} copy(f32[2,64]{1,0:T(2,128)} %get-tuple-element.19) | data formatting | bytes 1024
  62.6 1.4 %copy.17 = bf16[8,2048]{1,0:T(8,128)(2,1)} copy(bf16[8,2048]{1,0:T(8,128)(2,1)} %get-tuple-element.20) | data formatting | bytes 65536
Async XLA Ops:
  1.4 0.7 %copy-start.1 = (s32[192]{0:T(256)S(1)}, s32[192]{0:T(256)}, u32[]{:S(2)}) copy-start(s32[192]{0:T(256)} %slot_turbine.1) | copy-start | bytes 2308
  2.1 0.7 %copy-start.2 = (f32[4,64]{1,0:T(4,128)S(1)}, f32[4,64]{1,0:T(4,128)}, u32[]{:S(2)}) copy-start(f32[4,64]{1,0:T(4,128)} %rotors.1) | copy-start | bytes 3076
  2.7 0.7 %copy-start.3 = (s32[4]{0:T(128)S(1)}, s32[4]{0:T(128)}, u32[]{:S(2)}) copy-start(s32[4]{0:T(128)} %moved.1) | copy-start | bytes 52
  31.9 0.7 %copy-start = (f32[32,8,128]{2,1,0:T(8,128)}, f32[32,8,128]{2,1,0:T(8,128)S(1)}, u32[]{:S(2)}) copy-start(f32[32,8,128]{2,1,0:T(8,128)S(1)} %get-tuple-element.9.table_hbm.table) | copy-start | bytes 393220

commit v2 on v1

--- a/solution.py
+++ b/solution.py
@@ -15,6 +15,7 @@
 RECV = 8
 EDGE = 16
 CHUNK = 8
+STRIP = 48
 LANES = 128
 
 
@@ -26,30 +27,36 @@
 
 def sweep_plane(med, src, dst, prev, x, count):
     ahead = jnp.minimum(x + 1, count - 1)
-    inside = jnp.where(x + 1 < count, 1.0, 0.0)
-    viscous = med[0, x].astype(jnp.float32)
-    velocity = med[1, x].astype(jnp.float32)
-    reaction = med[2, x].astype(jnp.float32)
-    coupling = med[3, x].astype(jnp.float32)
-    source = med[4, x].astype(jnp.float32)
-    pull = (med[0, ahead].astype(jnp.float32) + med[1, ahead].astype(jnp.float32)) * inside
-    diagonal = 6.0 * viscous + velocity + reaction
-    rows, cols = viscous.shape
-    row = lax.broadcasted_iota(jnp.int32, (rows, cols), 0)
-    col = lax.broadcasted_iota(jnp.int32, (rows, cols), 1)
-    sides = []
-    for c in range(2):
-        flux = viscous * src[c, x]
-        total = prev[c] + pull * src[c, ahead]
-        prev[c] = flux
-        total = total + jnp.where(row == 0, 0.0, pltpu.roll(flux, 1, 0))
-        total = total + jnp.where(row == rows - 1, 0.0, pltpu.roll(flux, rows - 1, 0))
-        total = total + jnp.where(col == 0, 0.0, pltpu.roll(flux, 1, 1))
-        total = total + jnp.where(col == cols - 1, 0.0, pltpu.roll(flux, cols - 1, 1))
-        sides.append(total)
-    k, e = src[0, x], src[1, x]
-    dst[0, x] = k + TAU * (source + sides[0] - diagonal * k - coupling * e)
-    dst[1, x] = e + TAU * (sides[1] - (diagonal + reaction) * e - coupling * k)
+    inside = jnp.where(x + 1 < count, TAU, 0.0)
+    now, last = lax.rem(x, 2), 1 - lax.rem(x, 2)
+    rows, cols = src.shape[2:]
+    for start in range(0, rows, STRIP):
+        part = pl.ds(start, STRIP)
+        viscous = TAU * med[0, x, part].astype(jnp.float32)
+        for c in range(2):
+            prev[now, c, pl.ds(8 + start, STRIP)] = viscous * src[c, x, part]
+    col = lax.broadcasted_iota(jnp.int32, (STRIP, cols), 1)
+    for start in range(0, rows, STRIP):
+        part = pl.ds(start, STRIP)
+        scaled = TAU * med[2, x, part].astype(jnp.float32)
+        coupling = TAU * med[3, x, part].astype(jnp.float32)
+        pull = med[0, ahead, part].astype(jnp.float32) + med[1, ahead, part].astype(jnp.float32)
+        pull = pull * inside
+        keep = 1.0 - (6.0 * TAU) * med[0, x, part].astype(jnp.float32)
+        keep = keep - (TAU * med[1, x, part].astype(jnp.float32) + scaled)
+        values = src[0, x, part], src[1, x, part]
+        for c in range(2):
+            flux = prev[now, c, pl.ds(8 + start, STRIP)]
+            total = prev[last, c, pl.ds(8 + start, STRIP)] + pull * src[c, ahead, part]
+            total = total + jnp.where(col == 0, 0.0, pltpu.roll(flux, 1, 1))
+            total = total + jnp.where(col == cols - 1, 0.0, pltpu.roll(flux, cols - 1, 1))
+            total = total + prev[now, c, pl.ds(7 + start, STRIP)]
+            total = total + prev[now, c, pl.ds(9 + start, STRIP)]
+            if c == 0:
+                total = total + TAU * med[4, x, part].astype(jnp.float32)
+                dst[0, x, part] = keep * values[0] - coupling * values[1] + total
+            else:
+                dst[1, x, part] = (keep - scaled) * values[1] - coupling * values[0] + total
 
 
 def pack_tables(me, rotors, listed, moved, target, pack):
@@ -249,7 +256,7 @@
             for copy in chunk_in(i + 1):
                 copy.wait()
 
-        @pl.loop(0, CHUNK)
+        @pl.loop(0, CHUNK, unroll=2)
         def _(j):
             sweep_plane(med, q, q1, prev, i * CHUNK + j, count)
 
@@ -267,7 +274,7 @@
     outs = []
     for i in range(chunks):
 
-        @pl.loop(0, CHUNK)
+        @pl.loop(0, CHUNK, unroll=2)
         def _(j):
             sweep_plane(med, q1, q, prev, i * CHUNK + j, count)
 
@@ -310,7 +317,7 @@
             pltpu.VMEM(adjoint.shape, jnp.float32),
             pltpu.VMEM(medium.shape, jnp.bfloat16),
             pltpu.VMEM(adjoint.shape, jnp.float32),
-            pltpu.VMEM((channels, width, depth), jnp.float32),
+            pltpu.VMEM((2, channels, width + 16, depth), jnp.float32),
             pltpu.VMEM((2, 2, channels, width, depth), jnp.float32),
             pltpu.VMEM((2, 2, channels, width, depth), jnp.float32),
             pltpu.VMEM((2, 2, channels, count, depth), jnp.float32),
@@ -336,10 +343,10 @@
     z = np.arange(depth)[:, None] - np.arange(depth)[None, :]
     height = z + 0.5 - KZ / 2.0
     values = np.exp(-(height**2) / (2.0 * SIGMA_RADIAL**2)) * ((z >= 0) & (z < KZ))
-    values = values.astype(np.float32)
+    values = values.T.astype(np.float32)
     high = values.astype(jnp.bfloat16)
     low = (values - high.astype(np.float32)).astype(jnp.bfloat16)
-    return np.block([[high, low], [high, np.zeros_like(low)]])
+    return np.block([[high, high], [low, np.zeros_like(low)]])
 
 
 def slope_kernel(
@@ -353,6 +360,7 @@
     slopes,
     q,
     conv,
+    sums,
     table,
     table_sem,
     in_sem,
@@ -377,50 +385,49 @@
     for i in range(chunks):
         chunk_in(i).wait()
         chunk_out(i).start()
-        rows = q[0, pl.ds(i * CHUNK, CHUNK)].reshape(CHUNK * width, depth)
-        high = rows.astype(jnp.bfloat16)
-        low = (rows - high.astype(jnp.float32)).astype(jnp.bfloat16)
-        both = jnp.dot(
-            jnp.concatenate([high, low], axis=1),
-            profile[...],
-            preferred_element_type=jnp.float32,
-        )
-        conv[pl.ds(i * CHUNK, CHUNK)] = (both[:, :depth] + both[:, depth:]).reshape(
-            CHUNK, width, depth
-        )
+
+        @pl.loop(0, CHUNK, unroll=4)
+        def _(j):
+            x = i * CHUNK + j
+            plane = q[0, x]
+            high = plane.astype(jnp.bfloat16)
+            low = (plane - high.astype(jnp.float32)).astype(jnp.bfloat16)
+            both = lax.dot_general(
+                profile[...],
+                jnp.concatenate([high, low], axis=1),
+                (((1,), (1,)), ((), ())),
+                preferred_element_type=jnp.float32,
+            )
+            conv[pl.ds(x * depth, depth), pl.ds(0, width)] = both[:depth] + both[depth:]
 
     fetch.wait()
     slopes[...] = jnp.zeros_like(slopes)
     groups = -(-slots // LANES)
-    lane = lax.broadcasted_iota(jnp.int32, (1, LANES), 1)
-    wide = lax.broadcasted_iota(jnp.int32, (KX * KY, LANES), 1)
-    cell = lax.broadcasted_iota(jnp.int32, (KX * KY, LANES), 0)
-    cell_x = (cell // KY).astype(jnp.float32) + 0.5 - KX / 2.0
-    cell_y = lax.rem(cell, KY).astype(jnp.float32) + 0.5 - KY / 2.0
-    for group in range(groups):
-        start = group * LANES
-        stop = min(slots, start + LANES)
-
-        def gather(s, carry):
-            values, params = carry
+    shape = (KX, LANES)
+    lane = lax.broadcasted_iota(jnp.int32, shape, 1)
+    cell_x = lax.broadcasted_iota(jnp.int32, shape, 0).astype(jnp.float32) + 0.5 - KX / 2.0
+    cell_y = lax.rem(lane, KY).astype(jnp.float32) + 0.5 - KY / 2.0
+    share = LANES // KY
+    part = lax.div(lane, KY)
+
+    def line_of_slots(line, carry):
+        values = jnp.zeros(shape, jnp.float32)
+        fields = [jnp.zeros(shape, jnp.float32)] * 5
+        for j in range(share):
+            s = line * share + j
             turbine = jnp.maximum(slot_turbine[s], 0)
             first_x = jnp.minimum(corner[0, s], count - KX)
             first_y = jnp.minimum(corner[1, s], width - KY)
             first_z = jnp.minimum(corner[2, s], depth - KZ)
-            block = conv[pl.ds(first_x, KX), pl.ds(first_y, KY)].reshape(KX * KY, depth)
-            block = pltpu.roll(block, lax.rem(s - start - first_z + depth, depth), 1)
-            mine = lane == s - start
-            values = jnp.where(wide == s - start, block, values)
+            block = conv[pl.ds(first_x * depth + first_z, KX, depth), :]
+            block = pltpu.roll(block, lax.rem(j * KY - first_y + LANES, LANES), 1)
+            mine = part == j
+            values = jnp.where(mine, block, values)
             owner, local = lax.div(turbine, turb_dev), lax.rem(turbine, turb_dev)
-            params = tuple(
-                jnp.where(mine, table[owner, i, local], p) for i, p in enumerate(params)
-            )
-            return values, params
-
-        zero = jnp.zeros((1, LANES), jnp.float32)
-        values, (sub_x, sub_y, cosine, sine, thrust) = lax.fori_loop(
-            start, stop, gather, (jnp.zeros((KX * KY, LANES), jnp.float32), (zero,) * 5), unroll=2
-        )
+            fields = [
+                jnp.where(mine, table[owner, i, local], old) for i, old in enumerate(fields)
+            ]
+        sub_x, sub_y, cosine, sine, thrust = fields
         delta_x, delta_y = cell_x - sub_x, cell_y - sub_y
         along = cosine * delta_x + sine * delta_y
         across = cosine * delta_y - sine * delta_x
@@ -431,13 +438,34 @@
         weighted = kernel * values
         axial = along * (1.0 / (SIGMA_AXIAL * SIGMA_AXIAL))
         radial = across * (1.0 / (SIGMA_RADIAL * SIGMA_RADIAL))
-        other = groups + group
-        slopes[group : group + 1] = jnp.sum(
+        sums[0, pl.ds(line, 1)] = jnp.sum(
             weighted * (axial * cosine - radial * sine), axis=0, keepdims=True
         )
-        slopes[other : other + 1] = jnp.sum(
+        sums[1, pl.ds(line, 1)] = jnp.sum(
             weighted * (axial * sine + radial * cosine), axis=0, keepdims=True
         )
+        return carry
+
+    sums[...] = jnp.zeros_like(sums)
+    lax.fori_loop(0, slots // share, line_of_slots, 0, unroll=2)
+    spread = lax.div(lax.broadcasted_iota(jnp.int32, (LANES, LANES), 0), KY) == lax.rem(
+        lax.broadcasted_iota(jnp.int32, (LANES, LANES), 1), share
+    )
+    spread = jnp.where(spread, 1.0, 0.0)
+    lines = LANES // share
+    own = lax.div(lax.broadcasted_iota(jnp.int32, (lines, LANES), 1), share)
+    own = own == lax.broadcasted_iota(jnp.int32, (lines, LANES), 0)
+    for i in range(2):
+        total = jnp.dot(
+            sums[i],
+            spread,
+            precision=lax.Precision.HIGHEST,
+            preferred_element_type=jnp.float32,
+        )
+        for group in range(groups):
+            block = total[group * lines : (group + 1) * lines]
+            row = i * groups + group
+            slopes[row : row + 1] = jnp.sum(jnp.where(own, block, 0.0), axis=0, keepdims=True)
     for i in range(chunks):
         chunk_out(i).wait()
 
@@ -464,7 +492,8 @@
         ),
         scratch_shapes=[
             pltpu.VMEM(state.shape, jnp.float32),
-            pltpu.VMEM((count, width, depth), jnp.float32),
+            pltpu.VMEM((count * depth, LANES), jnp.float32),
+            pltpu.VMEM((2, -(-slot_turbine.shape[0] // LANES) * KY, LANES), jnp.float32),
             pltpu.SMEM(table.shape, jnp.float32),
             pltpu.SemaphoreType.DMA,
             pltpu.SemaphoreType.DMA((count // CHUNK,)),
@@ -475,14 +504,11 @@
     )(slot_turbine, slot_corner, table, state, jnp.asarray(z_weights(depth)))
 
 
-def finish_kernel(
-    sizes, groups, moved_dev, step_size, slopes, table, step_out, incoming, every, ssem, rsem
-):
+def share_kernel(sizes, slopes, out, every, ssem, rsem):
     n_gx, n_gy = sizes
     n = n_gx * n_gy
     gx, gy = lax.axis_index("gx"), lax.axis_index("gy")
     me = gx * n_gy + gy
-    turb_dev = step_out.shape[1]
     barrier = pltpu.get_barrier_semaphore()
 
     def peer(i):
@@ -510,39 +536,6 @@
         send(i).start()
 
     every[me] = slopes[...]
-
-    lines = table[:, 7]
-    lane = lax.broadcasted_iota(jnp.int32, lines.shape, 1)
-    mine = jnp.where((lines == me.astype(jnp.float32)) & (lane < moved_dev), 1.0, 0.0)
-
-    def earlier(size, row, col):
-        less = lax.broadcasted_iota(jnp.int32, (size, size), row) < lax.broadcasted_iota(
-            jnp.int32, (size, size), col
-        )
-        return jnp.where(less, 1.0, 0.0).astype(jnp.bfloat16)
-
-    rank = jnp.sum(
-        jnp.dot(
-            earlier(n, 1, 0), mine.astype(jnp.bfloat16), preferred_element_type=jnp.float32
-        ),
-        axis=1,
-        keepdims=True,
-    ) + jnp.dot(
-        mine.astype(jnp.bfloat16), earlier(LANES, 0, 1), preferred_element_type=jnp.float32
-    )
-    shifted = [pltpu.roll(lines, LANES - moved_dev * f, 1) for f in range(1, 7)]
-    chosen = [jnp.where(rank == float(slot), mine, 0.0) for slot in range(RECV)]
-
-    def per_slot(values):
-        parts = [jnp.sum(pick * values, axis=0, keepdims=True) for pick in chosen]
-        return jnp.sum(jnp.concatenate(parts, axis=0), axis=1, keepdims=True)
-
-    valid = per_slot(jnp.ones_like(lines))
-    wanted, sub_x, sub_y, cosine, sine, thrust = [per_slot(values) for values in shifted]
-    own = (
-        me * turb_dev + lax.broadcasted_iota(jnp.int32, (turb_dev, LANES), 0)
-    ).astype(jnp.float32)
-    targets = jnp.concatenate([own, jnp.broadcast_to(wanted, (RECV, LANES))], axis=0)
 
     @pl.loop(1, n)
     def _(i):
@@ -556,6 +549,47 @@
             device_id=peer(i),
             device_id_type=MESH,
         ).wait_recv()
+
+    out[...] = every[...]
+
+
+def finish_kernel(sizes, groups, moved_dev, step_size, every, table, step_out, incoming):
+    n = sizes[0] * sizes[1]
+    me = lax.axis_index("gx") * sizes[1] + lax.axis_index("gy")
+    turb_dev = step_out.shape[1]
+
+    lines = table[:, 7]
+    lane = lax.broadcasted_iota(jnp.int32, lines.shape, 1)
+    mine = jnp.where((lines == me.astype(jnp.float32)) & (lane < moved_dev), 1.0, 0.0)
+
+    def earlier(size, row, col):
+        less = lax.broadcasted_iota(jnp.int32, (size, size), row) < lax.broadcasted_iota(
+            jnp.int32, (size, size), col
+        )
+        return jnp.where(less, 1.0, 0.0).astype(jnp.bfloat16)
+
+    rank = jnp.sum(
+        jnp.dot(
+            earlier(n, 1, 0), mine.astype(jnp.bfloat16), preferred_element_type=jnp.float32
+        ),
+        axis=1,
+        keepdims=True,
+    ) + jnp.dot(
+        mine.astype(jnp.bfloat16), earlier(LANES, 0, 1), preferred_element_type=jnp.float32
+    )
+    shifted = [pltpu.roll(lines, LANES - moved_dev * f, 1) for f in range(1, 7)]
+    chosen = [jnp.where(rank == float(slot), mine, 0.0) for slot in range(RECV)]
+
+    def per_slot(values):
+        parts = [jnp.sum(pick * values, axis=0, keepdims=True) for pick in chosen]
+        return jnp.sum(jnp.concatenate(parts, axis=0), axis=1, keepdims=True)
+
+    valid = per_slot(jnp.ones_like(lines))
+    wanted, sub_x, sub_y, cosine, sine, thrust = [per_slot(values) for values in shifted]
+    own = (
+        me * turb_dev + lax.broadcasted_iota(jnp.int32, (turb_dev, LANES), 0)
+    ).astype(jnp.float32)
+    targets = jnp.concatenate([own, jnp.broadcast_to(wanted, (RECV, LANES))], axis=0)
 
     def collect(d, carry):
         sum_x, sum_y = carry
@@ -598,6 +632,19 @@
     n = sizes[0] * sizes[1]
     vmem = pl.BlockSpec(memory_space=pltpu.VMEM)
 
+    every = pl.pallas_call(
+        functools.partial(share_kernel, sizes),
+        out_shape=jax.ShapeDtypeStruct((n,) + slopes.shape, jnp.float32),
+        in_specs=[vmem],
+        out_specs=vmem,
+        scratch_shapes=[
+            pltpu.VMEM((n,) + slopes.shape, jnp.float32),
+            pltpu.SemaphoreType.DMA((n,)),
+            pltpu.SemaphoreType.DMA((n,)),
+        ],
+        compiler_params=pltpu.CompilerParams(collective_id=1, has_side_effects=True),
+        name="share",
+    )(slopes)
     return pl.pallas_call(
         functools.partial(finish_kernel, sizes, groups, moved_dev),
         out_shape=(
@@ -606,14 +653,8 @@
         ),
         in_specs=[pl.BlockSpec(memory_space=pltpu.SMEM), vmem, vmem],
         out_specs=(vmem, vmem),
-        scratch_shapes=[
-            pltpu.VMEM((n,) + slopes.shape, jnp.float32),
-            pltpu.SemaphoreType.DMA((n,)),
-            pltpu.SemaphoreType.DMA((n,)),
-        ],
-        compiler_params=pltpu.CompilerParams(collective_id=1, has_side_effects=True),
         name="finish",
-    )(step_size, slopes, table)
+    )(step_size, every, table)
 
 
 def body(

time: 64.2 us -> 56.4 us (0.88)
  Pallas kernels: 56.6 us -> 51.4 us
  local copies, waits for them, and re-layouts: 6.01 us -> 3.41 us
    pallas_call x0 -> x1, Pallas kernels: none -> 10.2 us  [finish(): pl.pallas_call(functools.partial(share_kernel, sizes), out_shape=jax.Shap...]
    pallas_call x1, Pallas kernels: 10.9 us -> 2.58 us  [finish(): pl.pallas_call(functools.partial(finish_kernel, sizes, groups, moved_dev)...]
    pallas_call x1, Pallas kernels: 17.2 us -> 11.5 us  [slot_slopes(): pl.pallas_call(functools.partial(slope_kernel, turb_dev), out_shape=(jax....]
    unnamed x11 -> x9, local copies, waits for them, and re-layouts: 6.01 us -> 3.41 us
    pallas_call x1, Pallas kernels: 28.5 us -> 27.2 us  [relax(): pl.pallas_call(functools.partial(relax_kernel, sizes), out_shape=(jax.Sha...]
where the time goes in v2:
time: 56.4 us; the launch traced here: 56.1 us
  Pallas kernels  51.4 us (91%)
  local copies, waits for them, and re-layouts  3.41 us (6%)
  between operations  1.31 us (2%)
    pallas_call x1, Pallas kernels, relax(): pl.pallas_call(functools.partial(relax_kernel, sizes), out_shape=(jax.Sha...  27.2 us
    pallas_call x1, Pallas kernels, slot_slopes(): pl.pallas_call(functools.partial(slope_kernel, turb_dev), out_shape=(jax....  11.5 us
    pallas_call x1, Pallas kernels, finish(): pl.pallas_call(functools.partial(share_kernel, sizes), out_shape=jax.Shap...  10.2 us
    unnamed x9, local copies, waits for them, and re-layouts  3.41 us
    pallas_call x1, Pallas kernels, finish(): pl.pallas_call(functools.partial(finish_kernel, sizes, groups, moved_dev)...  2.58 us

profile of v2, /device:TPU:0, one launch (start us, length us, event | category | flops | bytes accessed | tf_op | source)
XLA Modules:
  0.0 56.1 jit_solution(5731988730746100637)
XLA Ops:
  0.6 0.7 %copy.12.target = s32[4,1]{1,0:T(4,128)S(1)} copy(s32[4,1]{0,1:T(1,128)} %param.16) | data formatting | bytes 32 | tf_op args[7]
  1.4 0.0 copy-start.1
  1.4 0.7 %copy-done.1 = s32[192]{0:T(256)S(1)} copy-done((s32[192]{0:T(256)S(1)}, s32[192]{0:T(256)}, u32[]{:S(2)}) %copy-start.1) | copy-done | bytes 792
  2.1 0.0 copy-start.2
  2.1 0.7 %copy-done.2 = f32[4,64]{1,0:T(4,128)S(1)} copy-done((f32[4,64]{1,0:T(4,128)S(1)}, f32[4,64]{1,0:T(4,128)}, u32[]{:S(2)}) %copy-start.2) | copy-done | bytes 1048
  2.7 0.0 copy-start.3
  2.7 0.7 %copy-done.3 = s32[4]{0:T(128)S(1)} copy-done((s32[4]{0:T(128)S(1)}, s32[4]{0:T(128)}, u32[]{:S(2)}) %copy-start.3) | copy-done | bytes 40
  3.4 27.2 %relax.1 = (f32[2,64,96,128]{3,2,1,0:T(8,128)}, f32[32,8,128]{2,1,0:T(8,128)S(1)}) custom-call(f32[4,64]{1,0:T(4,128)S(1)} %copy-done.2, s32[1,192]{1,0:T(1,128)S(1)} %bitcast.3, s32[4]{0:T(128)S(1)} %copy-done.3, s32[4,1]{1,0:T(4,128)S(1)} %copy.12.target, f32[2,64,96,128]{3,2,1,0:T(8,128)} %q_hbm.1, bf16[5,64,96,128]{3,2,1,0:T(8,128)(2,1)} %med_hbm.1), custom_call_target="tpu_custom_call" | custom-call | tf_op jit(solution)/shard_map/relax/pallas_call | solution.py:308
  30.6 0.0 copy-start
  30.6 0.7 %copy-done = f32[32,8,128]{2,1,0:T(8,128)} copy-done((f32[32,8,128]{2,1,0:T(8,128)}, f32[32,8,128]{2,1,0:T(8,128)S(1)}, u32[]{:S(2)}) %copy-start) | copy-done | bytes 131096
  31.3 11.5 %slopes.1 = (f32[2,64,96,128]{3,2,1,0:T(8,128)}, f32[8,128]{1,0:T(8,128)}) custom-call(s32[192]{0:T(256)} %slot_turbine.1, s32[3,192]{1,0:T(4,128)} %corner.1, f32[32,8,128]{2,1,0:T(8,128)} %copy-done, f32[2,64,96,128]{3,2,1,0:T(8,128)} %get-tuple-element.10.q_hbm, bf16[256,256]{1,0:T(8,128)(2,1)} %constant.2.clone.profile), custom_call_target="tpu_custom_call" | custom-call | tf_op jit(solution)/shard_map/slopes/pallas_call | solution.py:476
  42.7 10.2 %share.1.every = f32[32,8,128]{2,1,0:T(8,128)} custom-call(f32[8,128]{1,0:T(8,128)} %get-tuple-element.12.slopes), custom_call_target="tpu_custom_call" | custom-call | tf_op jit(solution)/shard_map/share/pallas_call | solution.py:635
  53.5 2.6 %finish.1 = (f32[2,64]{1,0:T(2,128)}, bf16[8,2048]{1,0:T(8,128)(2,1)}) custom-call(f32[1]{0:T(128)} %bitcast.2.step_size, f32[32,8,128]{2,1,0:T(8,128)} %share.1.every, f32[32,8,128]{2,1,0:T(8,128)} %copy-done), custom_call_target="tpu_custom_call" | custom-call | tf_op jit(solution)/shard_map/finish/pallas_call | solution.py:648
Async XLA Ops:
  1.4 0.7 %copy-start.1 = (s32[192]{0:T(256)S(1)}, s32[192]{0:T(256)}, u32[]{:S(2)}) copy-start(s32[192]{0:T(256)} %slot_turbine.1) | copy-start | bytes 2308
  2.1 0.7 %copy-start.2 = (f32[4,64]{1,0:T(4,128)S(1)}, f32[4,64]{1,0:T(4,128)}, u32[]{:S(2)}) copy-start(f32[4,64]{1,0:T(4,128)} %rotors.1) | copy-start | bytes 3076
  2.7 0.7 %copy-start.3 = (s32[4]{0:T(128)S(1)}, s32[4]{0:T(128)}, u32[]{:S(2)}) copy-start(s32[4]{0:T(128)} %moved.1) | copy-start | bytes 52
  30.6 0.7 %copy-start = (f32[32,8,128]{2,1,0:T(8,128)}, f32[32,8,128]{2,1,0:T(8,128)S(1)}, u32[]{:S(2)}) copy-start(f32[32,8,128]{2,1,0:T(8,128)S(1)} %get-tuple-element.9.table_hbm.table) | copy-start | bytes 393220

commit v3 on v2

--- a/solution.py
+++ b/solution.py
@@ -89,6 +89,54 @@
     pack[7:8] = line
 
 
+def greet(sizes):
+    n_gx, n_gy = sizes
+    gx, gy = lax.axis_index("gx"), lax.axis_index("gy")
+    barrier = pltpu.get_barrier_semaphore()
+    for j in range(1, n_gy):
+        pl.semaphore_signal(
+            barrier, inc=1, device_id=(gx, lax.rem(gy + j, n_gy)), device_id_type=MESH
+        )
+    for j in range(1, n_gx):
+        pl.semaphore_signal(
+            barrier, inc=1, device_id=(lax.rem(gx + j, n_gx), gy), device_id_type=MESH
+        )
+    return n_gx + n_gy - 2
+
+
+def spread_y(sizes, own, every, ssem, rsem):
+    n_gy = sizes[1]
+    gx, gy = lax.axis_index("gx"), lax.axis_index("gy")
+    return [
+        pltpu.make_async_remote_copy(
+            src_ref=own,
+            dst_ref=every.at[gx * n_gy + gy],
+            send_sem=ssem.at[j],
+            recv_sem=rsem.at[j],
+            device_id=(gx, lax.rem(gy + j, n_gy)),
+            device_id_type=MESH,
+        )
+        for j in range(1, n_gy)
+    ]
+
+
+def spread_x(sizes, every, ssem, rsem):
+    n_gx, n_gy = sizes
+    gx, gy = lax.axis_index("gx"), lax.axis_index("gy")
+    block = every.at[pl.ds(gx * n_gy, n_gy)]
+    return [
+        pltpu.make_async_remote_copy(
+            src_ref=block,
+            dst_ref=block,
+            send_sem=ssem.at[n_gy + j],
+            recv_sem=rsem.at[n_gy + j],
+            device_id=(lax.rem(gx + j, n_gx), gy),
+            device_id_type=MESH,
+        )
+        for j in range(1, n_gx)
+    ]
+
+
 def relax_kernel(
     sizes,
     rotors,
@@ -118,7 +166,6 @@
     trecv,
 ):
     n_gx, n_gy = sizes
-    n = n_gx * n_gy
     _, count, width, _ = q.shape
     chunks = count // CHUNK
     gx, gy = lax.axis_index("gx"), lax.axis_index("gy")
@@ -154,29 +201,9 @@
     barrier = pltpu.get_barrier_semaphore()
     me = gx * n_gy + gy
 
-    @pl.loop(1, n)
-    def _(i):
-        other = lax.rem(me + i, n)
-        pl.semaphore_signal(
-            barrier,
-            inc=1,
-            device_id=(lax.div(other, n_gy), lax.rem(other, n_gy)),
-            device_id_type=MESH,
-        )
-
+    met = greet(sizes)
     pack_tables(me, rotors, listed, moved, target, pack)
-    pl.semaphore_wait(barrier, n - 1)
-
-    def share(i, place):
-        other = lax.rem(me + i, n)
-        return pltpu.make_async_remote_copy(
-            src_ref=pack,
-            dst_ref=table.at[place],
-            send_sem=tsend.at[i],
-            recv_sem=trecv.at[place],
-            device_id=(lax.div(other, n_gy), lax.rem(other, n_gy)),
-            device_id_type=MESH,
-        )
+    pl.semaphore_wait(barrier, met)
 
     def exchange(turn, src):
         for c in range(2):
@@ -245,11 +272,10 @@
 
     copies = exchange(0, q)
 
-    @pl.loop(1, n)
-    def _(i):
-        share(i, me).start()
-
     table[me] = pack[...]
+    along_y = spread_y(sizes, pack, table, tsend, trecv)
+    for copy in along_y:
+        copy.start()
     prev[...] = jnp.zeros_like(prev)
     for i in range(chunks):
         if 0 < i + 1 < chunks - 1:
@@ -265,6 +291,11 @@
     patch(0, q1)
 
     copies = exchange(1, q1)
+    for copy in along_y:
+        copy.wait()
+    along_x = spread_x(sizes, table, tsend, trecv)
+    for copy in along_x:
+        copy.start()
     prev[...] = jnp.zeros_like(prev)
 
     def chunk_out(i):
@@ -282,11 +313,8 @@
             outs.append(chunk_out(i))
             outs[-1].start()
 
-    @pl.loop(1, n)
-    def _(i):
-        share(i, me).wait_send()
-        share(i, lax.rem(me + i, n)).wait_recv()
-
+    for copy in along_x:
+        copy.wait()
     every[...] = table[...]
     for copy in copies:
         copy.wait()
@@ -329,8 +357,8 @@
             pltpu.SemaphoreType.DMA((2 + count // CHUNK,)),
             pltpu.SemaphoreType.DMA((2, 4)),
             pltpu.SemaphoreType.DMA((2, 4)),
-            pltpu.SemaphoreType.DMA((n,)),
-            pltpu.SemaphoreType.DMA((n,)),
+            pltpu.SemaphoreType.DMA((sizes[0] + sizes[1],)),
+            pltpu.SemaphoreType.DMA((sizes[0] + sizes[1],)),
         ],
         compiler_params=pltpu.CompilerParams(
             collective_id=0, has_side_effects=True, vmem_limit_bytes=48 * 1024 * 1024
@@ -505,51 +533,19 @@
 
 
 def share_kernel(sizes, slopes, out, every, ssem, rsem):
-    n_gx, n_gy = sizes
-    n = n_gx * n_gy
-    gx, gy = lax.axis_index("gx"), lax.axis_index("gy")
-    me = gx * n_gy + gy
-    barrier = pltpu.get_barrier_semaphore()
-
-    def peer(i):
-        other = lax.rem(me + i, n)
-        return (lax.div(other, n_gy), lax.rem(other, n_gy))
-
-    @pl.loop(1, n)
-    def _(i):
-        pl.semaphore_signal(barrier, inc=1, device_id=peer(i), device_id_type=MESH)
-
-    pl.semaphore_wait(barrier, n - 1)
-
-    def send(i):
-        return pltpu.make_async_remote_copy(
-            src_ref=slopes,
-            dst_ref=every.at[me],
-            send_sem=ssem.at[i],
-            recv_sem=rsem.at[me],
-            device_id=peer(i),
-            device_id_type=MESH,
-        )
-
-    @pl.loop(1, n)
-    def _(i):
-        send(i).start()
-
-    every[me] = slopes[...]
-
-    @pl.loop(1, n)
-    def _(i):
-        send(i).wait_send()
-        other = lax.rem(me + i, n)
-        pltpu.make_async_remote_copy(
-            src_ref=slopes,
-            dst_ref=every.at[other],
-            send_sem=ssem.at[i],
-            recv_sem=rsem.at[other],
-            device_id=peer(i),
-            device_id_type=MESH,
-        ).wait_recv()
-
+    met = greet(sizes)
+    every[lax.axis_index("gx") * sizes[1] + lax.axis_index("gy")] = slopes[...]
+    pl.semaphore_wait(pltpu.get_barrier_semaphore(), met)
+    along_y = spread_y(sizes, slopes, every, ssem, rsem)
+    for copy in along_y:
+        copy.start()
+    for copy in along_y:
+        copy.wait()
+    along_x = spread_x(sizes, every, ssem, rsem)
+    for copy in along_x:
+        copy.start()
+    for copy in along_x:
+        copy.wait()
     out[...] = every[...]
 
 
@@ -639,8 +635,8 @@
         out_specs=vmem,
         scratch_shapes=[
             pltpu.VMEM((n,) + slopes.shape, jnp.float32),
-            pltpu.SemaphoreType.DMA((n,)),
-            pltpu.SemaphoreType.DMA((n,)),
+            pltpu.SemaphoreType.DMA((sizes[0] + sizes[1],)),
+            pltpu.SemaphoreType.DMA((sizes[0] + sizes[1],)),
         ],
         compiler_params=pltpu.CompilerParams(collective_id=1, has_side_effects=True),
         name="share",

time: 56.4 us -> 55.5 us (0.984)
  Pallas kernels: 51.4 us -> 50.5 us
    pallas_call x1, Pallas kernels: 27.2 us -> 25.2 us  [relax(): pl.pallas_call(functools.partial(relax_kernel, sizes), out_shape=(jax.Sha...]
    pallas_call x1, Pallas kernels: 10.2 us -> 11.3 us  [finish(): pl.pallas_call(functools.partial(share_kernel, sizes), out_shape=jax.Shap...]
where the time goes in v3:
time: 55.5 us; the launch traced here: 55.2 us
  Pallas kernels  50.5 us (91%)
  local copies, waits for them, and re-layouts  3.41 us (6%)
  between operations  1.31 us (2%)
    pallas_call x1, Pallas kernels, relax(): pl.pallas_call(functools.partial(relax_kernel, sizes), out_shape=(jax.Sha...  25.2 us
    pallas_call x1, Pallas kernels, slot_slopes(): pl.pallas_call(functools.partial(slope_kernel, turb_dev), out_shape=(jax....  11.5 us
    pallas_call x1, Pallas kernels, finish(): pl.pallas_call(functools.partial(share_kernel, sizes), out_shape=jax.Shap...  11.3 us
    unnamed x9, local copies, waits for them, and re-layouts  3.41 us
    pallas_call x1, Pallas kernels, finish(): pl.pallas_call(functools.partial(finish_kernel, sizes, groups, moved_dev)...  2.58 us

profile of v3, /device:TPU:0, one launch (start us, length us, event | category | flops | bytes accessed | tf_op | source)
XLA Modules:
  0.0 55.2 jit_solution(16324709426543149752)
XLA Ops:
  0.6 0.7 %copy.12.target = s32[4,1]{1,0:T(4,128)S(1)} copy(s32[4,1]{0,1:T(1,128)} %param.16) | data formatting | bytes 32 | tf_op args[7]
  1.4 0.0 copy-start.1
  1.4 0.7 %copy-done.1 = s32[192]{0:T(256)S(1)} copy-done((s32[192]{0:T(256)S(1)}, s32[192]{0:T(256)}, u32[]{:S(2)}) %copy-start.1) | copy-done | bytes 792
  2.1 0.0 copy-start.2
  2.1 0.7 %copy-done.2 = f32[4,64]{1,0:T(4,128)S(1)} copy-done((f32[4,64]{1,0:T(4,128)S(1)}, f32[4,64]{1,0:T(4,128)}, u32[]{:S(2)}) %copy-start.2) | copy-done | bytes 1048
  2.7 0.0 copy-start.3
  2.7 0.7 %copy-done.3 = s32[4]{0:T(128)S(1)} copy-done((s32[4]{0:T(128)S(1)}, s32[4]{0:T(128)}, u32[]{:S(2)}) %copy-start.3) | copy-done | bytes 40
  3.4 25.2 %relax.1 = (f32[2,64,96,128]{3,2,1,0:T(8,128)}, f32[32,8,128]{2,1,0:T(8,128)S(1)}) custom-call(f32[4,64]{1,0:T(4,128)S(1)} %copy-done.2, s32[1,192]{1,0:T(1,128)S(1)} %bitcast.3, s32[4]{0:T(128)S(1)} %copy-done.3, s32[4,1]{1,0:T(4,128)S(1)} %copy.12.target, f32[2,64,96,128]{3,2,1,0:T(8,128)} %q_hbm.1, bf16[5,64,96,128]{3,2,1,0:T(8,128)(2,1)} %med_hbm.1), custom_call_target="tpu_custom_call" | custom-call | tf_op jit(solution)/shard_map/relax/pallas_call | solution.py:336
  28.5 0.0 copy-start
  28.6 0.7 %copy-done = f32[32,8,128]{2,1,0:T(8,128)} copy-done((f32[32,8,128]{2,1,0:T(8,128)}, f32[32,8,128]{2,1,0:T(8,128)S(1)}, u32[]{:S(2)}) %copy-start) | copy-done | bytes 131096
  29.2 11.5 %slopes.1 = (f32[2,64,96,128]{3,2,1,0:T(8,128)}, f32[8,128]{1,0:T(8,128)}) custom-call(s32[192]{0:T(256)} %slot_turbine.1, s32[3,192]{1,0:T(4,128)} %corner.1, f32[32,8,128]{2,1,0:T(8,128)} %copy-done, f32[2,64,96,128]{3,2,1,0:T(8,128)} %get-tuple-element.10.q_hbm, bf16[256,256]{1,0:T(8,128)(2,1)} %constant.2.clone.profile), custom_call_target="tpu_custom_call" | custom-call | tf_op jit(solution)/shard_map/slopes/pallas_call | solution.py:504
  40.7 11.3 %share.1.every = f32[32,8,128]{2,1,0:T(8,128)} custom-call(f32[8,128]{1,0:T(8,128)} %get-tuple-element.12.slopes), custom_call_target="tpu_custom_call" | custom-call | tf_op jit(solution)/shard_map/share/pallas_call | solution.py:631
  52.6 2.6 %finish.1 = (f32[2,64]{1,0:T(2,128)}, bf16[8,2048]{1,0:T(8,128)(2,1)}) custom-call(f32[1]{0:T(128)} %bitcast.2.step_size, f32[32,8,128]{2,1,0:T(8,128)} %share.1.every, f32[32,8,128]{2,1,0:T(8,128)} %copy-done), custom_call_target="tpu_custom_call" | custom-call | tf_op jit(solution)/shard_map/finish/pallas_call | solution.py:644
Async XLA Ops:
  1.4 0.7 %copy-start.1 = (s32[192]{0:T(256)S(1)}, s32[192]{0:T(256)}, u32[]{:S(2)}) copy-start(s32[192]{0:T(256)} %slot_turbine.1) | copy-start | bytes 2308
  2.1 0.7 %copy-start.2 = (f32[4,64]{1,0:T(4,128)S(1)}, f32[4,64]{1,0:T(4,128)}, u32[]{:S(2)}) copy-start(f32[4,64]{1,0:T(4,128)} %rotors.1) | copy-start | bytes 3076
  2.7 0.7 %copy-start.3 = (s32[4]{0:T(128)S(1)}, s32[4]{0:T(128)}, u32[]{:S(2)}) copy-start(s32[4]{0:T(128)} %moved.1) | copy-start | bytes 52
  28.5 0.7 %copy-start = (f32[32,8,128]{2,1,0:T(8,128)}, f32[32,8,128]{2,1,0:T(8,128)S(1)}, u32[]{:S(2)}) copy-start(f32[32,8,128]{2,1,0:T(8,128)S(1)} %get-tuple-element.9.table_hbm.table) | copy-start | bytes 393220
